TPU v7x, 512 devices: a whole 4x4x16 slice. The times are simulated.
512 devices in a mesh: group: 8 (over z_lo), shard: 64 (over z_hi, x, y, core).
Axes of the slice: x: 4, y: 4, z: 16 (z_hi: 2, z_lo: 8; z = z_hi * 8 + z_lo), core: 2. Of those that a mesh axis runs over, the one named last changes fastest.
Arguments:
- inner_embed: float32 [8, 15360, 768], P('group', 'shard'), may hold values from -6 to 6
- outer_embed: float32 [15360, 768], P('shard'), may hold values from -6 to 6
- moment_embed: float32 [15360, 768], P('shard'), may hold values from -6 to 6
- basis: float32 [15360, 64], P('shard'), may hold values from -6 to 6
- inner_attn: float32 [8, 768, 3072], P('group', 'shard'), may hold values from -6 to 6
- outer_attn: float32 [768, 3072], P(None, 'shard'), may hold values from -6 to 6
- moment_attn: float32 [768, 3072], P(None, 'shard'), may hold values from -6 to 6
- inner_norms: float32 [8, 4, 768], P('group', None, 'shard'), may hold values from -6 to 6
- outer_norms: float32 [4, 768], P(None, 'shard'), may hold values from -6 to 6
- moment_norms: float32 [4, 768], P(None, 'shard'), may hold values from -6 to 6
Outputs:
- new_embed: float32 [15360, 768], P('shard')
- new_moment_embed: float32 [15360, 768], P('shard')
- new_attn: float32 [768, 3072], P(None, 'shard')
- new_moment_attn: float32 [768, 3072], P(None, 'shard')
- new_norms: float32 [4, 768], P(None, 'shard')
- new_moment_norms: float32 [4, 768], P(None, 'shard')
- replica_attn: bfloat16 [768, 3072], P('shard')
All inputs are finite; a program needn't handle non-finite values.
Results may differ from a plain program's by a relative error of at most 0.0004.
Values may be sent and summed in bfloat16 or wider, within the bound.
A program may use at most 64 MiB of HBM per device.

v0:
```python
import math
import jax
import jax.numpy as jnp
from jax import lax
from jax.sharding import PartitionSpec as P

VOCAB = 15360
RANK = 64


def nesterov(outer, moment, delta):
    moment_new = 0.5 * moment + delta
    return (outer - (delta + 0.5 * moment_new), moment_new)


def on_device(
    inner_embed,
    outer_embed,
    moment_embed,
    basis,
    inner_attn,
    outer_attn,
    moment_attn,
    inner_norms,
    outer_norms,
    moment_norms,
):
    groups = lax.axis_size("group")
    embed_diff = outer_embed - inner_embed[0]
    partial_coeff = lax.dot_general(
        basis,
        embed_diff,
        (((0,), (0,)), ((), ())),
        precision=lax.Precision.HIGHEST,
        preferred_element_type=jnp.float32,
    )
    norm_diff = outer_norms - inner_norms[0]
    moved = lax.all_to_all(inner_attn[0], "shard", split_axis=1, concat_axis=0, tiled=True)
    attn_term = outer_attn - moved
    coeff_sum = lax.psum(partial_coeff, ("group", "shard"))
    attn_sum, norm_sum = lax.psum((attn_term, norm_diff), "group")
    attn_delta = attn_sum / groups
    norm_delta = norm_sum / groups
    coefficient = coeff_sum / groups
    embed_delta = jnp.dot(
        basis, coefficient, precision=lax.Precision.HIGHEST, preferred_element_type=jnp.float32
    ) * (1.0 / math.sqrt(RANK * VOCAB))
    new_embed, new_moment_embed = nesterov(outer_embed, moment_embed, embed_delta)
    new_attn, new_moment_attn = nesterov(outer_attn, moment_attn, attn_delta)
    new_norms, new_moment_norms = nesterov(outer_norms, moment_norms, norm_delta)
    replica_attn = lax.all_to_all(
        new_attn.astype(jnp.bfloat16), "shard", split_axis=0, concat_axis=1, tiled=True
    )
    return (
        new_embed,
        new_moment_embed,
        new_attn,
        new_moment_attn,
        new_norms,
        new_moment_norms,
        replica_attn,
    )


def solution(mesh):
    placed = (
        P("group", "shard", None),
        P("shard", None),
        P("shard", None),
        P("shard", None),
        P("group", "shard", None),
        P(None, "shard"),
        P(None, "shard"),
        P("group", None, "shard"),
        P(None, "shard"),
        P(None, "shard"),
    )
    return jax.shard_map(
        on_device,
        mesh=mesh,
        in_specs=placed,
        out_specs=(
            P("shard", None),
            P("shard", None),
            P(None, "shard"),
            P(None, "shard"),
            P(None, "shard"),
            P(None, "shard"),
            P("shard", None),
        ),
        check_vma=False,
    )
```

profile of v0, /device:TPU:1, one launch (start us, length us, event | category | flops | bytes accessed | tf_op | source)
XLA Modules:
  0.0 638.4 jit_solution(14730503204910227283)
XLA Ops:
  7.2 0.0 copy-start
  7.2 1.3 reduce
  8.5 0.2 all_to_all.28
  8.7 0.2 copy.34
  8.9 1.0 reshape.22
  9.9 0.0 copy-start.4
  9.9 22.4 %all-to-all-start = ((f32[64,1,576]{2,1,0:T(1,128)}), f32[64,1,576]{2,1,0:T(1,128)S(1)}, u32[]{:S(2)}, u32[]{:S(2)}) async-start(f32[64,1,576]{2,1,0:T(1,128)} %reshape.22), calls=%async_computation | async-start | bytes 327680 | tf_op jit(solution)/shard_map/all_to_all | solution.py:38
  32.3 0.0 all-reduce.5.cloned.1.call-start
  32.4 0.0 copy-done.4
  32.4 0.2 copy.29
  32.6 17.3 %all-to-all-done = f32[64,1,576]{2,1,0:T(1,128)S(1)} async-done(((f32[64,1,576]{2,1,0:T(1,128)}), f32[64,1,576]{2,1,0:T(1,128)S(1)}, u32[]{:S(2)}, u32[]{:S(2)}) %all-to-all-start) | async-done | bytes 147488 | tf_op jit(solution)/shard_map/all_to_all | solution.py:38
  49.9 0.5 broadcast.29
  50.4 1.0 reduce.1
  51.4 0.2 reshape.23
  51.7 0.0 copy-start.1
  51.7 0.0 copy-start.2
  51.7 0.8 sub.20
  52.5 0.0 all-reduce.5.cloned.1.call-update
  52.5 0.0 all-reduce.3.cloned.1.call-start
  52.6 0.0 copy-done
  52.6 0.4 copy-done.1
  53.0 0.2 copy-done.2
  53.2 1.3 convolution_bitcast_fusion
  54.5 0.0 copy-start.5
  54.5 0.0 all-reduce.3.cloned.1.call-update
  54.5 0.9 copy-done.5
  55.4 0.0 copy-start.6
  55.4 0.2 copy.28
  55.5 0.5 copy-done.6
  56.1 0.0 copy-done.7
  56.1 27.7 %psum.23 = f32[4,12]{1,0:T(4,128)S(1)} all-reduce(f32[4,12]{1,0:T(4,128)S(1)} %bitcast_subtract_fusion.2), channel_id=1, replica_groups=mesh['group'=8,'shard'=64] {'group'}, use_global_device_ids=true, to_apply=%region_2.0 | all-reduce | flops 48 | bytes 384 | tf_op jit(solution)/shard_map/psum | solution.py:41
  83.8 0.0 copy-done.8
  83.8 0.6 add_subtract_fusion.2
  84.4 80.6 %all-reduce.5.cloned.1.call-done = f32[768,48]{1,0:T(8,128)} async-done(((f32[768,48]{1,0:T(8,128)}), f32[768,48]{1,0:T(8,128)}) %all-reduce.5.cloned.1.call-update) | async-done | bytes 147472 | tf_op jit(solution)/shard_map/psum | solution.py:41
  165.0 1.1 fusion.4
  166.1 0.0 copy-start.3
  166.1 0.1 all_to_all.32
  166.2 0.9 reshape.24
  167.1 16.1 %all-to-all-start.1 = ((bf16[64,2,288]{2,1,0:T(2,128)(2,1)}), bf16[64,2,288]{2,1,0:T(2,128)(2,1)S(1)}, u32[]{:S(2)}, u32[]{:S(2)}) async-start(bf16[64,2,288]{2,1,0:T(2,128)(2,1)} %reshape.24), calls=%async_computation.1 | async-start | bytes 196608 | tf_op jit(solution)/shard_map/all_to_all | solution.py:51
  183.3 442.5 %all-reduce.3.cloned.1.call-done = f32[64,768]{1,0:T(8,128)} async-done(((f32[64,768]{1,0:T(8,128)}), f32[64,768]{1,0:T(8,128)}) %all-reduce.3.cloned.1.call-update) | async-done | bytes 196624 | tf_op jit(solution)/shard_map/psum | solution.py:40
  625.8 0.0 copy-done.3
  625.8 2.9 add_subtract_fusion
  628.7 0.8 copy.31
  629.5 0.8 copy.32
  630.3 0.0 all-to-all-done.1
  630.3 0.2 reshape.25
  630.6 0.1 copy.30
  630.6 0.9 all_to_all.35
  (5 shorter events, 0.1 us)
Async XLA Ops:
  7.2 45.4 %copy-start = (f32[240,64]{0,1:T(8,128)S(1)}, f32[240,64]{0,1:T(8,128)}, u32[]{:S(2)}) copy-start(f32[240,64]{0,1:T(8,128)} %param.13) | copy-start | bytes 184324
  9.9 22.4 %copy-start.4 = (f32[768,48]{0,1:T(8,128)S(1)}, f32[768,48]{0,1:T(8,128)}, u32[]{:S(2)}) copy-start(f32[768,48]{0,1:T(8,128)} %param.15) | copy-start | bytes 442372
  9.9 39.9 %all-to-all-start = ((f32[64,1,576]{2,1,0:T(1,128)}), f32[64,1,576]{2,1,0:T(1,128)S(1)}, u32[]{:S(2)}, u32[]{:S(2)}) async-start(f32[64,1,576]{2,1,0:T(1,128)} %reshape.22), calls=%async_computation | async-start | bytes 327680 | tf_op jit(solution)/shard_map/all_to_all | solution.py:38
  32.3 132.7 %all-reduce.5.cloned.1.call-start = ((), (), s32[]{:S(2)}) async-start(), calls=%async_computation.3 | async-start | bytes 786432 | tf_op jit(solution)/shard_map/psum | solution.py:41
  51.7 1.3 copy-start.1
  51.7 1.5 copy-start.2
  52.5 573.3 %all-reduce.3.cloned.1.call-start = ((), (), s32[]{:S(2)}) async-start(), calls=%async_computation.2 | async-start | bytes 393216 | tf_op jit(solution)/shard_map/psum | solution.py:40
  54.5 0.9 copy-start.5
  55.4 0.7 copy-start.6
  55.4 0.7 copy-start.7
  56.1 27.7 %copy-start.8 = (f32[4,12]{1,0:T(4,128)S(1)}, f32[4,12]{1,0:T(4,128)}, u32[]{:S(2)}) copy-start(f32[4,12]{1,0:T(4,128)} %param.19) | copy-start | bytes 580
  166.1 459.7 %copy-start.3 = (f32[240,768]{1,0:T(8,128)S(1)}, f32[240,768]{1,0:T(8,128)}, u32[]{:S(2)}) copy-start(f32[240,768]{1,0:T(8,128)} %param.12) | copy-start | bytes 2211844
  167.1 463.2 %all-to-all-start.1 = ((bf16[64,2,288]{2,1,0:T(2,128)(2,1)}), bf16[64,2,288]{2,1,0:T(2,128)(2,1)S(1)}, u32[]{:S(2)}, u32[]{:S(2)}) async-start(bf16[64,2,288]{2,1,0:T(2,128)(2,1)} %reshape.24), calls=%async_computation.1 | async-start | bytes 196608 | tf_op jit(solution)/shard_map/all_to_all | solution.py:51
Sparse Core Ops, SparseCore 0:
  52.7 112.3 all-reduce.4
  171.9 453.8 all-reduce.2
where the time goes:
time: 639 us; the launch traced here: 638 us
  waiting for transfers between devices  540 us (85%)
  starting transfers between devices  38.6 us (6%)
  blocking collectives  27.7 us (4%)
  between operations  14.2 us (2%)
  local copies, waits for them, and re-layouts  8.4 us (1%)
    psum x1, waiting for transfers between devices, on_device(): coeff_sum = lax.psum(partial_coeff, ('group', 'shard'))  442 us
    psum x1, waiting for transfers between devices, on_device(): attn_sum, norm_sum = lax.psum((attn_term, norm_diff), 'group')  80.6 us
    psum x1, blocking collectives, on_device(): attn_sum, norm_sum = lax.psum((attn_term, norm_diff), 'group')  27.7 us
    all_to_all x1, starting transfers between devices, on_device(): lax.all_to_all(inner_attn[0], 'shard', split_axis=1, concat_axis=0, tiled...  22.4 us
    all_to_all x1, waiting for transfers between devices, on_device(): lax.all_to_all(inner_attn[0], 'shard', split_axis=1, concat_axis=0, tiled...  17.3 us
    all_to_all x1, starting transfers between devices, on_device(): lax.all_to_all(new_attn.astype(jnp.bfloat16), 'shard', split_axis=0, conc...  16.1 us
  transfers between devices with their start and end apart: 4, of which 3 were waited for; matrix products, arithmetic and copies ran while one was open for 1% of the time, Pallas kernels for 0%

commit v1 on v0

--- a/solution.py
+++ b/solution.py
@@ -35,7 +35,10 @@
         preferred_element_type=jnp.float32,
     )
     norm_diff = outer_norms - inner_norms[0]
-    moved = lax.all_to_all(inner_attn[0], "shard", split_axis=1, concat_axis=0, tiled=True)
+    own = inner_attn[0]
+    shards = jnp.split(own, lax.axis_size("shard"), axis=1)
+    arrived = lax.all_to_all(jnp.stack(shards), "shard", 0, 0)
+    moved = jnp.concatenate(arrived, axis=0)
     attn_term = outer_attn - moved
     coeff_sum = lax.psum(partial_coeff, ("group", "shard"))
     attn_sum, norm_sum = lax.psum((attn_term, norm_diff), "group")

time: 639 us -> 653 us (1.022)
  waiting for transfers between devices: 540 us -> 548 us
    psum x1, waiting for transfers between devices: 442 us -> 452 us  [on_device(): coeff_sum = lax.psum(partial_coeff, ('group', 'shard'))]
where the time goes in v1:
time: 653 us; the launch traced here: 651 us
  waiting for transfers between devices  548 us (84%)
  starting transfers between devices  38.6 us (6%)
  blocking collectives  28.5 us (4%)
  between operations  14.2 us (2%)
  local copies, waits for them, and re-layouts  13.1 us (2%)
    psum x1, waiting for transfers between devices, on_device(): coeff_sum = lax.psum(partial_coeff, ('group', 'shard'))  452 us
    psum x1, waiting for transfers between devices, on_device(): attn_sum, norm_sum = lax.psum((attn_term, norm_diff), 'group')  79.1 us
    psum x1, blocking collectives, on_device(): attn_sum, norm_sum = lax.psum((attn_term, norm_diff), 'group')  28.5 us
    all_to_all x1, starting transfers between devices, on_device(): arrived = lax.all_to_all(jnp.stack(shards), 'shard', 0, 0)  22.4 us
    all_to_all x1, waiting for transfers between devices, on_device(): arrived = lax.all_to_all(jnp.stack(shards), 'shard', 0, 0)  17.3 us
    all_to_all x1, starting transfers between devices, on_device(): lax.all_to_all(new_attn.astype(jnp.bfloat16), 'shard', split_axis=0, conc...  16.1 us
  transfers between devices with their start and end apart: 4, of which 3 were waited for; matrix products, arithmetic and copies ran while one was open for 1% of the time, Pallas kernels for 0%

profile of v1, /device:TPU:1, one launch (start us, length us, event | category | flops | bytes accessed | tf_op | source)
XLA Modules:
  0.0 651.3 jit_solution(12243828588606453239)
XLA Ops:
  7.2 1.0 copy.27
  8.2 0.1 constant_dynamic-update-slice_fusion.62
  8.2 0.1 constant_dynamic-update-slice_fusion.61
  8.3 0.1 constant_dynamic-update-slice_fusion.60
  8.4 0.1 constant_dynamic-update-slice_fusion.59
  8.5 0.1 constant_dynamic-update-slice_fusion.58
  9.0 0.1 constant_dynamic-update-slice_fusion.50
  9.1 0.1 constant_dynamic-update-slice_fusion.48
  9.4 0.1 constant_dynamic-update-slice_fusion.43
  9.6 0.1 constant_dynamic-update-slice_fusion.41
  9.8 0.1 constant_dynamic-update-slice_fusion.36
  10.3 0.1 constant_dynamic-update-slice_fusion.29
  10.7 0.1 constant_dynamic-update-slice_fusion.24
  10.7 0.1 constant_dynamic-update-slice_fusion.22
  11.1 0.1 constant_dynamic-update-slice_fusion.17
  11.2 0.1 constant_dynamic-update-slice_fusion.14
  11.3 0.1 constant_dynamic-update-slice_fusion.13
  11.5 0.1 constant_dynamic-update-slice_fusion.10
  11.7 0.1 constant_dynamic-update-slice_fusion.8
  11.8 0.1 constant_dynamic-update-slice_fusion.6
  11.8 0.1 constant_dynamic-update-slice_fusion.5
  11.9 0.1 constant_dynamic-update-slice_fusion.4
  12.3 1.1 reshape.21
  13.4 22.4 %all-to-all-start = ((f32[64,1,576]{2,1,0:T(1,128)}), f32[64,1,576]{2,1,0:T(1,128)S(1)}, u32[]{:S(2)}, u32[]{:S(2)}) async-start(f32[64,1,576]{2,1,0:T(1,128)} %reshape.21), calls=%async_computation | async-start | bytes 327680 | tf_op jit(solution)/shard_map/all_to_all | solution.py:40
  35.8 0.2 copy.21
  36.0 17.3 %all-to-all-done = f32[64,1,576]{2,1,0:T(1,128)S(1)} async-done(((f32[64,1,576]{2,1,0:T(1,128)}), f32[64,1,576]{2,1,0:T(1,128)S(1)}, u32[]{:S(2)}, u32[]{:S(2)}) %all-to-all-start) | async-done | bytes 147488 | tf_op jit(solution)/shard_map/all_to_all | solution.py:40
  53.3 0.5 broadcast.28
  53.8 1.0 reduce
  54.8 0.2 reshape.22
  55.1 0.8 sub.20
  56.0 0.4 copy-done.1
  56.4 0.2 copy-done.3
  56.6 2.2 convolution_bitcast_fusion
  58.8 0.9 copy-done.5
  59.7 0.2 copy.20
  59.8 0.5 copy-done.6
  60.4 28.5 %psum.23 = f32[4,12]{1,0:T(4,128)S(1)} all-reduce(f32[4,12]{1,0:T(4,128)S(1)} %bitcast_subtract_fusion.2), channel_id=1, replica_groups=mesh['group'=8,'shard'=64] {'group'}, use_global_device_ids=true, to_apply=%region_2.0 | all-reduce | flops 48 | bytes 384 | tf_op jit(solution)/shard_map/psum | solution.py:44
  88.8 0.6 add_subtract_fusion.2
  89.4 79.1 %all-reduce.5.cloned.1.call-done = f32[768,48]{1,0:T(8,128)} async-done(((f32[768,48]{1,0:T(8,128)}), f32[768,48]{1,0:T(8,128)}) %all-reduce.5.cloned.1.call-update) | async-done | bytes 147472 | tf_op jit(solution)/shard_map/psum | solution.py:44
  168.5 1.1 fusion.4
  169.7 0.9 reshape.23
  170.6 16.1 %all-to-all-start.1 = ((bf16[64,2,288]{2,1,0:T(2,128)(2,1)}), bf16[64,2,288]{2,1,0:T(2,128)(2,1)S(1)}, u32[]{:S(2)}, u32[]{:S(2)}) async-start(bf16[64,2,288]{2,1,0:T(2,128)(2,1)} %reshape.23), calls=%async_computation.1 | async-start | bytes 196608 | tf_op jit(solution)/shard_map/all_to_all | solution.py:54
  186.8 451.9 %all-reduce.3.cloned.1.call-done = f32[64,768]{0,1:T(8,128)} async-done(((f32[64,768]{0,1:T(8,128)}), f32[64,768]{0,1:T(8,128)}) %all-reduce.3.cloned.1.call-update) | async-done | bytes 196624 | tf_op jit(solution)/shard_map/psum | solution.py:43
  638.7 3.0 add_subtract_fusion
  641.7 0.8 copy.23
  642.5 0.8 copy.24
  643.3 0.2 reshape.24
  643.6 0.9 all_to_all.21
  (66 shorter events, 2.9 us)
Async XLA Ops:
  7.2 48.8 %copy-start = (f32[240,64]{0,1:T(8,128)S(1)}, f32[240,64]{0,1:T(8,128)}, u32[]{:S(2)}) copy-start(f32[240,64]{0,1:T(8,128)} %param.13) | copy-start | bytes 184324
  13.4 22.4 %copy-start.4 = (f32[768,48]{0,1:T(8,128)S(1)}, f32[768,48]{0,1:T(8,128)}, u32[]{:S(2)}) copy-start(f32[768,48]{0,1:T(8,128)} %param.15) | copy-start | bytes 442372
  13.4 39.9 %all-to-all-start = ((f32[64,1,576]{2,1,0:T(1,128)}), f32[64,1,576]{2,1,0:T(1,128)S(1)}, u32[]{:S(2)}, u32[]{:S(2)}) async-start(f32[64,1,576]{2,1,0:T(1,128)} %reshape.21), calls=%async_computation | async-start | bytes 327680 | tf_op jit(solution)/shard_map/all_to_all | solution.py:40
  35.8 132.7 %all-reduce.5.cloned.1.call-start = ((), (), s32[]{:S(2)}) async-start(), calls=%async_computation.3 | async-start | bytes 786432 | tf_op jit(solution)/shard_map/psum | solution.py:44
  55.1 1.3 copy-start.1
  55.1 1.5 copy-start.3
  55.9 582.8 %all-reduce.3.cloned.1.call-start = ((), (), s32[]{:S(2)}) async-start(), calls=%async_computation.2 | async-start | bytes 786432 | tf_op jit(solution)/shard_map/psum | solution.py:43
  58.7 0.9 copy-start.5
  59.6 0.7 copy-start.6
  59.7 0.7 copy-start.7
  60.4 28.5 %copy-start.8 = (f32[4,12]{1,0:T(4,128)S(1)}, f32[4,12]{1,0:T(4,128)}, u32[]{:S(2)}) copy-start(f32[4,12]{1,0:T(4,128)} %param.19) | copy-start | bytes 580
  169.6 469.1 %copy-start.2 = (f32[240,768]{1,0:T(8,128)S(1)}, f32[240,768]{1,0:T(8,128)}, u32[]{:S(2)}) copy-start(f32[240,768]{1,0:T(8,128)} %param.12) | copy-start | bytes 2211844
  170.6 472.7 %all-to-all-start.1 = ((bf16[64,2,288]{2,1,0:T(2,128)(2,1)}), bf16[64,2,288]{2,1,0:T(2,128)(2,1)S(1)}, u32[]{:S(2)}, u32[]{:S(2)}) async-start(bf16[64,2,288]{2,1,0:T(2,128)(2,1)} %reshape.23), calls=%async_computation.1 | async-start | bytes 196608 | tf_op jit(solution)/shard_map/all_to_all | solution.py:54
Sparse Core Ops, SparseCore 0:
  56.0 112.4 all-reduce.4
  175.3 463.3 all-reduce.2

commit v2 on v0

--- a/solution.py
+++ b/solution.py
@@ -37,7 +37,8 @@
     norm_diff = outer_norms - inner_norms[0]
     moved = lax.all_to_all(inner_attn[0], "shard", split_axis=1, concat_axis=0, tiled=True)
     attn_term = outer_attn - moved
-    coeff_sum = lax.psum(partial_coeff, ("group", "shard"))
+    one_axis = lax.psum(partial_coeff, "group")
+    coeff_sum = lax.psum(one_axis, "shard")
     attn_sum, norm_sum = lax.psum((attn_term, norm_diff), "group")
     attn_delta = attn_sum / groups
     norm_delta = norm_sum / groups

time: 639 us -> 1200 us (1.88)
  waiting for transfers between devices: 540 us -> 1100 us
    psum x2, waiting for transfers between devices: 523 us -> 1090 us  [the longest x1 1000 us: on_device(): coeff_sum = lax.psum(one_axis, 'shard')]
where the time goes in v2:
time: 1200 us
  waiting for transfers between devices  1100 us (92%)
  starting transfers between devices  38.3 us (3%)
  blocking collectives  27.9 us (2%)
  between operations  14.2 us (1%)
    psum x1, waiting for transfers between devices, on_device(): coeff_sum = lax.psum(one_axis, 'shard')  1000 us
    psum x1, waiting for transfers between devices, on_device(): one_axis = lax.psum(partial_coeff, 'group')  85.4 us
    psum x1, blocking collectives, on_device(): attn_sum, norm_sum = lax.psum((attn_term, norm_diff), 'group')  27.9 us
  transfers between devices with their start and end apart: 4, of which 3 were waited for; matrix products, arithmetic and copies ran while one was open for 1% of the time, Pallas kernels for 0%

profile of v2, /device:TPU:1, one launch (start us, length us, event | category | flops | bytes accessed | tf_op | source)
XLA Modules:
  0.0 1200.6 jit_solution(12373521406950182621)
XLA Ops:
  7.2 0.0 copy-start
  7.2 1.3 reduce
  8.5 0.2 all_to_all.28
  8.7 0.2 copy.34
  8.9 0.0 copy-start.4
  8.9 0.0 copy-start.5
  8.9 0.0 copy-start.2
  8.9 1.0 reshape.22
  10.0 0.0 copy-start.1
  10.0 22.4 %all-to-all-start = ((f32[64,1,576]{2,1,0:T(1,128)}), f32[64,1,576]{2,1,0:T(1,128)S(1)}, u32[]{:S(2)}, u32[]{:S(2)}) async-start(f32[64,1,576]{2,1,0:T(1,128)} %reshape.22), calls=%async_computation | async-start | bytes 327680 | tf_op jit(solution)/shard_map/all_to_all | solution.py:38
  32.4 0.0 all-reduce.6.cloned.1.call-start
  32.4 0.0 copy-done.4
  32.4 0.2 copy.29
  32.6 0.0 copy-done.5
  32.6 0.2 copy.28
  32.8 0.0 copy-done
  32.8 0.0 copy-done.2
  32.8 0.0 copy-done.1
  32.8 1.3 convolution_bitcast_fusion
  34.1 15.8 %all-to-all-done = f32[64,1,576]{2,1,0:T(1,128)S(1)} async-done(((f32[64,1,576]{2,1,0:T(1,128)}), f32[64,1,576]{2,1,0:T(1,128)S(1)}, u32[]{:S(2)}, u32[]{:S(2)}) %all-to-all-start) | async-done | bytes 147488 | tf_op jit(solution)/shard_map/all_to_all | solution.py:38
  49.9 0.5 broadcast.29
  50.4 1.0 reduce.1
  51.4 0.2 reshape.23
  51.7 0.8 sub.20
  52.5 0.0 copy-start.6
  52.5 0.0 all-reduce.6.cloned.1.call-update
  52.5 0.0 all-reduce.4.cloned.1.call-start
  52.6 0.6 copy-done.6
  53.2 0.0 copy-done.7
  53.2 27.9 %psum.31 = f32[4,12]{1,0:T(4,128)S(1)} all-reduce(f32[4,12]{1,0:T(4,128)S(1)} %bitcast_subtract_fusion.2), channel_id=1, replica_groups=mesh['group'=8,'shard'=64] {'group'}, use_global_device_ids=true, to_apply=%region_3.0 | all-reduce | flops 48 | bytes 384 | tf_op jit(solution)/shard_map/psum | solution.py:42
  81.2 0.0 copy-done.8
  81.2 0.6 add_subtract_fusion.2
  81.7 85.4 %all-reduce.6.cloned.1.call-done = (f32[64,768]{1,0:T(8,128)}, f32[768,48]{1,0:T(8,128)}) async-done(((f32[64,768]{1,0:T(8,128)}, f32[768,48]{1,0:T(8,128)}), (f32[64,768]{1,0:T(8,128)}, f32[768,48]{1,0:T(8,128)})) %all-reduce.6.cloned.1.call-update) | async-done | bytes 344080 | tf_op jit(solution)/shard_map/psum | solution.py:40
  167.2 0.0 all-reduce.4.cloned.1.call-update
  167.2 1.1 fusion.4
  168.3 0.1 all_to_all.32
  168.4 0.0 copy-start.3
  168.4 0.9 reshape.24
  169.3 15.8 %all-to-all-start.1 = ((bf16[64,2,288]{2,1,0:T(2,128)(2,1)}), bf16[64,2,288]{2,1,0:T(2,128)(2,1)S(1)}, u32[]{:S(2)}, u32[]{:S(2)}) async-start(bf16[64,2,288]{2,1,0:T(2,128)(2,1)} %reshape.24), calls=%async_computation.1 | async-start | bytes 196608 | tf_op jit(solution)/shard_map/all_to_all | solution.py:52
  185.2 0.8 copy.31
  186.0 0.8 copy.32
  186.8 1002.8 %all-reduce.4.cloned.1.call-done = f32[64,768]{1,0:T(8,128)} async-done(((f32[64,768]{1,0:T(8,128)}), f32[64,768]{1,0:T(8,128)}) %all-reduce.4.cloned.1.call-update) | async-done | bytes 196624 | tf_op jit(solution)/shard_map/psum | solution.py:41
  1189.6 0.0 copy-done.3
  1189.6 2.9 add_subtract_fusion
  1192.5 0.0 all-to-all-done.1
  1192.5 0.2 reshape.25
  1192.7 0.1 copy.30
  1192.8 0.9 all_to_all.35
  (5 shorter events, 0.1 us)
Async XLA Ops:
  7.2 25.6 %copy-start = (f32[240,64]{0,1:T(8,128)S(1)}, f32[240,64]{0,1:T(8,128)}, u32[]{:S(2)}) copy-start(f32[240,64]{0,1:T(8,128)} %param.13) | copy-start | bytes 184324
  8.9 23.5 %copy-start.4 = (f32[768,48]{0,1:T(8,128)S(1)}, f32[768,48]{0,1:T(8,128)}, u32[]{:S(2)}) copy-start(f32[768,48]{0,1:T(8,128)} %param.15) | copy-start | bytes 442372
  8.9 23.7 %copy-start.5 = (f32[768,48]{0,1:T(8,128)S(1)}, f32[768,48]{0,1:T(8,128)}, u32[]{:S(2)}) copy-start(f32[768,48]{0,1:T(8,128)} %param.16) | copy-start | bytes 442372
  8.9 23.8 %copy-start.2 = (f32[1,240,768]{2,1,0:T(8,128)S(1)}, f32[1,240,768]{2,1,0:T(8,128)}, u32[]{:S(2)}) copy-start(f32[1,240,768]{2,1,0:T(8,128)} %param.10) | copy-start | bytes 2211844
  10.0 22.8 %copy-start.1 = (f32[240,768]{1,0:T(8,128)S(1)}, f32[240,768]{1,0:T(8,128)}, u32[]{:S(2)}) copy-start(f32[240,768]{1,0:T(8,128)} %param.11) | copy-start | bytes 2211844
  10.0 39.9 %all-to-all-start = ((f32[64,1,576]{2,1,0:T(1,128)}), f32[64,1,576]{2,1,0:T(1,128)S(1)}, u32[]{:S(2)}, u32[]{:S(2)}) async-start(f32[64,1,576]{2,1,0:T(1,128)} %reshape.22), calls=%async_computation | async-start | bytes 327680 | tf_op jit(solution)/shard_map/all_to_all | solution.py:38
  32.4 134.8 %all-reduce.6.cloned.1.call-start = ((), (), s32[]{:S(2)}) async-start(), calls=%async_computation.3 | async-start | bytes 1179648 | tf_op jit(solution)/shard_map/psum | solution.py:40
  52.5 0.7 copy-start.6
  52.5 0.7 copy-start.7
  52.5 1137.0 %all-reduce.4.cloned.1.call-start = ((), (), s32[]{:S(2)}) async-start(), calls=%async_computation.2 | async-start | bytes 393216 | tf_op jit(solution)/shard_map/psum | solution.py:41
  53.2 27.9 %copy-start.8 = (f32[4,12]{1,0:T(4,128)S(1)}, f32[4,12]{1,0:T(4,128)}, u32[]{:S(2)}) copy-start(f32[4,12]{1,0:T(4,128)} %param.19) | copy-start | bytes 580
  168.4 1021.2 %copy-start.3 = (f32[240,768]{1,0:T(8,128)S(1)}, f32[240,768]{1,0:T(8,128)}, u32[]{:S(2)}) copy-start(f32[240,768]{1,0:T(8,128)} %param.12) | copy-start | bytes 2211844
  169.3 1023.2 %all-to-all-start.1 = ((bf16[64,2,288]{2,1,0:T(2,128)(2,1)}), bf16[64,2,288]{2,1,0:T(2,128)(2,1)S(1)}, u32[]{:S(2)}, u32[]{:S(2)}) async-start(bf16[64,2,288]{2,1,0:T(2,128)(2,1)} %reshape.24), calls=%async_computation.1 | async-start | bytes 196608 | tf_op jit(solution)/shard_map/all_to_all | solution.py:52
Sparse Core Ops, SparseCore 0:
  52.7 114.4 all-reduce.5
  170.1 1019.4 all-reduce.3
